TPU v7x, 32 devices: a whole 2x2x4 slice. The times are simulated.
32 devices in a mesh: row: 8 (over y, x, core), col: 4 (over z).
Axes of the slice: x: 2, y: 2, z: 4, core: 2. Of those that a mesh axis runs over, the one named last changes fastest.
Arguments:
- pair: bfloat16 [64, 64, 128], P('row', 'col'), may hold values from -6 to 6
- pair_mask: int32 [64, 64], P('row', 'col'), may hold values 0 or 1
- ln_in_gain: float32 [128], replicated, may hold values from 0.1 to 1.9
- ln_in_bias: float32 [128], replicated, may hold values from -3 to 3
- w_proj: bfloat16 [128, 512], replicated, may hold values from -0.5 to 0.5
- b_proj: float32 [512], replicated, may hold values from -3 to 3
- w_gate: bfloat16 [128, 128], replicated, may hold values from -0.5 to 0.5
- b_gate: float32 [128], replicated, may hold values from -3 to 3
- ln_mid_gain: float32 [128], replicated, may hold values from 0.1 to 1.9
- ln_mid_bias: float32 [128], replicated, may hold values from -3 to 3
- w_out: bfloat16 [128, 128], replicated, may hold values from -0.5 to 0.5
- b_out: float32 [128], replicated, may hold values from -3 to 3
- cotangent: bfloat16 [64, 64, 128], P('row', 'col'), may hold values from -6 to 6
Outputs:
- update: bfloat16 [64, 64, 128], P('row', 'col')
- pair_grad: float32 [64, 64, 128], P('row', 'col')
All inputs are finite; a program needn't handle non-finite values. No bound on the sum of `pair_mask` on one device may be relied on, other than what follows from the above.
Results may differ from a plain program's by a relative error of at most 0.019.
Values may be sent and summed in bfloat16 or wider, within the bound.
A program may use at most 64 MiB of HBM per device.

v0:
```python
import jax
import jax.numpy as jnp
from jax import lax
from jax.sharding import PartitionSpec as P


def layer_norm(values, gain_vec, bias_vec):
    average = jnp.mean(values, -1, keepdims=True)
    centred = values - average
    inv_std = lax.rsqrt(jnp.mean(centred * centred, -1, keepdims=True) + 1e-05)
    hat_val = centred * inv_std
    return (hat_val * gain_vec + bias_vec, hat_val, inv_std)


def norm_back(upstream, hat_val, inv_std, gain_vec):
    scaled = upstream * gain_vec
    return inv_std * (
        scaled
        - jnp.mean(scaled, -1, keepdims=True)
        - hat_val * jnp.mean(scaled * hat_val, -1, keepdims=True)
    )


def gate_pair(proj, mask_f):
    hidden = proj.shape[-1] // 4
    sig_a = jax.nn.sigmoid(proj[..., :hidden])
    sig_b = jax.nn.sigmoid(proj[..., 2 * hidden : 3 * hidden])
    a_bf = (mask_f * sig_a * proj[..., hidden : 2 * hidden]).astype(jnp.bfloat16)
    b_bf = (mask_f * sig_b * proj[..., 3 * hidden :]).astype(jnp.bfloat16)
    return (a_bf, b_bf)


def gate_back(grad_a, grad_b, proj, mask_f):
    hidden = proj.shape[-1] // 4
    sig_a = jax.nn.sigmoid(proj[..., :hidden])
    val_a = proj[..., hidden : 2 * hidden]
    sig_b = jax.nn.sigmoid(proj[..., 2 * hidden : 3 * hidden])
    val_b = proj[..., 3 * hidden :]
    masked_a = grad_a * mask_f
    masked_b = grad_b * mask_f
    return jnp.concatenate(
        [
            masked_a * val_a * sig_a * (1.0 - sig_a),
            masked_a * sig_a,
            masked_b * val_b * sig_b * (1.0 - sig_b),
            masked_b * sig_b,
        ],
        -1,
    )


def per_device(
    pair,
    pair_mask,
    ln_in_gain,
    ln_in_bias,
    w_proj,
    b_proj,
    w_gate,
    b_gate,
    ln_mid_gain,
    ln_mid_bias,
    w_out,
    b_out,
    cotangent,
):
    normed, hat_in, rstd_in = layer_norm(pair.astype(jnp.float32), ln_in_gain, ln_in_bias)
    x_bf = normed.astype(jnp.bfloat16)
    proj = jnp.dot(x_bf, w_proj, preferred_element_type=jnp.float32) + b_proj
    mask_f = pair_mask.astype(jnp.float32)[..., None]
    a_bf, b_bf = gate_pair(proj, mask_f)
    b_every = lax.all_gather(b_bf, "row", axis=0, tiled=True)
    owned = lax.psum_scatter(
        jnp.einsum("jkh,ikh->jih", b_every, a_bf, preferred_element_type=jnp.float32).astype(
            jnp.bfloat16
        ),
        "col",
        scatter_dimension=0,
        tiled=True,
    ).astype(jnp.float32)
    triangle = jnp.transpose(owned, (1, 0, 2))
    mid_val, hat_mid, rstd_mid = layer_norm(triangle, ln_mid_gain, ln_mid_bias)
    mid_bf = mid_val.astype(jnp.bfloat16)
    out_lin = jnp.dot(mid_bf, w_out, preferred_element_type=jnp.float32) + b_out
    gate = jax.nn.sigmoid(jnp.dot(x_bf, w_gate, preferred_element_type=jnp.float32) + b_gate)
    update = (gate * out_lin).astype(jnp.bfloat16)
    grad_out = cotangent.astype(jnp.float32)
    d_out = (grad_out * gate).astype(jnp.bfloat16)
    d_gpre = (grad_out * out_lin * gate * (1.0 - gate)).astype(jnp.bfloat16)
    d_mid = jnp.dot(d_out, w_out.T, preferred_element_type=jnp.float32)
    d_tri = norm_back(d_mid, hat_mid, rstd_mid, ln_mid_gain).astype(jnp.bfloat16)
    tri_rows = lax.all_gather(d_tri, "col", axis=1, tiled=True)
    grad_a = jnp.einsum("ijh,jkh->ikh", tri_rows, b_every, preferred_element_type=jnp.float32)
    grad_b = lax.psum_scatter(
        jnp.einsum("ijh,ikh->jkh", tri_rows, a_bf, preferred_element_type=jnp.float32).astype(
            jnp.bfloat16
        ),
        "row",
        scatter_dimension=0,
        tiled=True,
    ).astype(jnp.float32)
    d_proj = gate_back(grad_a, grad_b, proj, mask_f).astype(jnp.bfloat16)
    d_x = jnp.dot(d_proj, w_proj.T, preferred_element_type=jnp.float32) + jnp.dot(
        d_gpre, w_gate.T, preferred_element_type=jnp.float32
    )
    pair_grad = norm_back(d_x, hat_in, rstd_in, ln_in_gain)
    return (update, pair_grad)


def solution(mesh):
    placed = (
        P("row", "col", None),
        P("row", "col"),
        P(),
        P(),
        P(),
        P(),
        P(),
        P(),
        P(),
        P(),
        P(),
        P(),
        P("row", "col", None),
    )
    return jax.shard_map(
        per_device,
        mesh=mesh,
        in_specs=placed,
        out_specs=(P("row", "col", None), P("row", "col", None)),
        check_vma=False,
    )
```

profile of v0, /device:TPU:0, one launch (start us, length us, event | category | flops | bytes accessed | tf_op | source)
XLA Modules:
  0.0 108.7 jit_solution(9767718973377871491)
XLA Ops:
  7.2 0.7 convert_element_type.52
  7.9 0.8 convert_reduce_fusion
  8.8 0.9 fusion.26
  9.8 1.0 convolution_add_fusion
  10.9 10.8 %all_gather.6 = bf16[64,16,128]{2,1,0:T(8,128)(2,1)S(1)} all-gather(bf16[8,16,128]{2,1,0:T(8,128)(2,1)S(1)} %get-tuple-element.12), channel_id=1, replica_groups=mesh['row'=8,'col'=4] {'row'}, dimensions={0}, use_global_device_ids=true | all-gather | bytes 294912 | tf_op jit(solution)/shard_map/all_gather | solution.py:72
  21.8 3.0 %copy.24 = bf16[64,16,128]{1,0,2:T(8,128)(2,1)S(1)} copy(bf16[64,16,128]{2,1,0:T(8,128)(2,1)S(1)} %all_gather.6) | data formatting | bytes 524288 | tf_op jit(solution)/shard_map/all_gather | solution.py:72
  24.9 1.2 %fusion = bf16[64,8,128]{0,1,2:T(8,128)(2,1)S(1)} fusion(bf16[8,16,128]{1,0,2:T(8,128)(2,1)S(1)} %copy.23, bf16[64,16,128]{1,0,2:T(8,128)(2,1)S(1)} %copy.24), kind=kOutput, calls=%fused_computation.1 | convolution fusion | flops 2162688 | bytes 425984 | tf_op jit(solution)/shard_map/jkh,ikh->jih/dot_general | solution.py:74
  26.1 0.9 copy.25
  27.0 19.6 %reduce-scatter.3.cloned.1.call-done = bf16[16,8,128]{2,1,0:T(8,128)(2,1)} async-done(((bf16[64,8,128]{2,1,0:T(8,128)(2,1)}), bf16[16,8,128]{2,1,0:T(8,128)(2,1)}) %reduce-scatter.3.cloned.1.call-update) | async-done | bytes 32784 | tf_op jit(solution)/shard_map/reduce_scatter | solution.py:73
  46.7 0.8 bitcast_reduce_fusion
  47.5 0.9 fusion.48
  48.5 1.0 convolution_add_fusion.2
  49.5 0.9 multiply_convert_fusion.4
  50.4 1.0 fusion.67
  51.4 0.9 fusion.47
  52.4 13.4 %all_gather.7 = bf16[8,64,128]{2,0,1:T(8,128)(2,1)S(1)} all-gather(bf16[8,16,128]{2,0,1:T(8,128)(2,1)S(1)} %copy.27), channel_id=1, replica_groups=mesh['row'=8,'col'=4] {'col'}, dimensions={1}, use_global_device_ids=true | all-gather | bytes 163840 | tf_op jit(solution)/shard_map/all_gather | solution.py:92
  65.8 0.2 copy.29
  66.0 0.4 fusion.69
  66.4 1.3 %copy.33 = bf16[128,16,64]{0,1,2:T(8,128)(2,1)} copy(bf16[128,16,64]{2,1,0:T(8,128)(2,1)S(1)} %fusion.69) | data formatting | bytes 524288 | tf_op jit(solution)/shard_map/ijh,ikh->jkh/dot_general | solution.py:95
  67.7 0.7 fusion.68
  68.6 31.1 %reduce-scatter.5.cloned.1.call-done = bf16[8,16,128]{2,1,0:T(8,128)(2,1)} async-done(((bf16[64,16,128]{2,1,0:T(8,128)(2,1)}), bf16[8,16,128]{2,1,0:T(8,128)(2,1)}) %reduce-scatter.5.cloned.1.call-update) | async-done | bytes 32784 | tf_op jit(solution)/shard_map/reduce_scatter | solution.py:94
  99.7 0.9 multiply_convert_fusion.3
  100.8 0.3 fusion.66
  101.1 0.8 fusion.25
  (52 shorter events, 0.9 us)
Async XLA Ops:
  7.2 2.6 %copy-start = (bf16[128,512]{1,0:T(8,128)(2,1)S(1)}, bf16[128,512]{1,0:T(8,128)(2,1)}, u32[]{:S(2)}) copy-start(bf16[128,512]{1,0:T(8,128)(2,1)} %param.17) | copy-start | bytes 393220
  7.2 39.5 %reduce-scatter.3.cloned.1.call-start = ((), (), s32[]{:S(2)}) async-start(), calls=%async_computation.2 | async-start | bytes 163840 | tf_op jit(solution)/shard_map/reduce_scatter | solution.py:73
  24.8 23.7 %copy-start.9 = (bf16[128,128]{1,0:T(8,128)(2,1)S(1)}, bf16[128,128]{1,0:T(8,128)(2,1)}, u32[]{:S(2)}) copy-start(bf16[128,128]{1,0:T(8,128)(2,1)} %param.23) | copy-start | bytes 98308
  24.8 23.7 %copy-start.14 = (f32[128]{0:T(128)S(1)}, f32[128]{0:T(128)}, u32[]{:S(2)}) copy-start(f32[128]{0:T(128)} %param.21) | copy-start | bytes 1540
  24.8 23.7 %copy-start.15 = (f32[128]{0:T(128)S(1)}, f32[128]{0:T(128)}, u32[]{:S(2)}) copy-start(f32[128]{0:T(128)} %param.24) | copy-start | bytes 1540
  24.8 23.7 %copy-start.16 = (f32[128]{0:T(128)S(1)}, f32[128]{0:T(128)}, u32[]{:S(2)}) copy-start(f32[128]{0:T(128)} %param.22) | copy-start | bytes 1540
  24.8 24.6 %copy-start.1 = (bf16[8,16,128]{2,1,0:T(8,128)(2,1)S(1)}, bf16[8,16,128]{2,1,0:T(8,128)(2,1)}, u32[]{:S(2)}) copy-start(bf16[8,16,128]{2,1,0:T(8,128)(2,1)} %param.13) | copy-start | bytes 98308
  24.9 24.6 %copy-start.10 = (bf16[128,128]{1,0:T(8,128)(2,1)S(1)}, bf16[128,128]{1,0:T(8,128)(2,1)}, u32[]{:S(2)}) copy-start(bf16[128,128]{1,0:T(8,128)(2,1)} %param.19) | copy-start | bytes 98308
  24.9 24.6 %copy-start.12 = (f32[128]{0:T(128)S(1)}, f32[128]{0:T(128)}, u32[]{:S(2)}) copy-start(f32[128]{0:T(128)} %param.15) | copy-start | bytes 1540
  24.9 24.6 %copy-start.13 = (f32[128]{0:T(128)S(1)}, f32[128]{0:T(128)}, u32[]{:S(2)}) copy-start(f32[128]{0:T(128)} %param.16) | copy-start | bytes 1540
  24.9 24.6 %copy-start.17 = (f32[128]{0:T(128)S(1)}, f32[128]{0:T(128)}, u32[]{:S(2)}) copy-start(f32[128]{0:T(128)} %param.20) | copy-start | bytes 1540
  24.9 25.5 %copy-start.5 = (bf16[8,16,128]{2,1,0:T(8,128)(2,1)S(1)}, bf16[8,16,128]{2,1,0:T(8,128)(2,1)}, u32[]{:S(2)}) copy-start(bf16[8,16,128]{2,1,0:T(8,128)(2,1)} %param.25) | copy-start | bytes 98308
  27.0 72.7 %reduce-scatter.5.cloned.1.call-start = ((), (), s32[]{:S(2)}) async-start(), calls=%async_computation.3 | async-start | bytes 294912 | tf_op jit(solution)/shard_map/reduce_scatter | solution.py:94
  49.5 0.9 copy-start.7
  50.4 2.0 %copy-start.3 = (f32[8,16,128]{2,1,0:T(8,128)}, f32[8,16,128]{2,1,0:T(8,128)S(1)}, u32[]{:S(2)}) copy-start(f32[8,16,128]{2,1,0:T(8,128)S(1)} %get-tuple-element.15) | copy-start | bytes 196612
  67.7 33.0 %copy-start.2 = (bf16[8,16,128]{2,1,0:T(8,128)(2,1)S(1)}, bf16[8,16,128]{2,1,0:T(8,128)(2,1)}, u32[]{:S(2)}) copy-start(bf16[8,16,128]{2,1,0:T(8,128)(2,1)} %param.13) | copy-start | bytes 98308
  67.7 33.0 %copy-start.4 = (f32[8,16,128]{2,1,0:T(8,128)S(1)}, f32[8,16,128]{2,1,0:T(8,128)}, u32[]{:S(2)}) copy-start(f32[8,16,128]{2,1,0:T(8,128)} %copy-done.3) | copy-start | bytes 196612
  67.7 33.0 %copy-start.6 = (bf16[8,16,128]{2,1,0:T(8,128)(2,1)S(1)}, bf16[8,16,128]{2,1,0:T(8,128)(2,1)}, u32[]{:S(2)}) copy-start(bf16[8,16,128]{2,1,0:T(8,128)(2,1)} %param.25) | copy-start | bytes 98308
  67.7 33.0 %copy-start.8 = (f32[8,16,128]{2,1,0:T(8,128)S(1)}, f32[8,16,128]{2,1,0:T(8,128)}, u32[]{:S(2)}) copy-start(f32[8,16,128]{2,1,0:T(8,128)} %copy-done.7) | copy-start | bytes 196612
  67.7 33.0 %copy-start.11 = (bf16[128,128]{1,0:T(8,128)(2,1)S(1)}, bf16[128,128]{1,0:T(8,128)(2,1)}, u32[]{:S(2)}) copy-start(bf16[128,128]{1,0:T(8,128)(2,1)} %param.19) | copy-start | bytes 98308
Sparse Core Ops, SparseCore 0:
  27.1 19.4 reduce-scatter.2
  67.8 31.8 reduce-scatter.4
where the time goes:
time: 109 us
  waiting for transfers between devices  50.7 us (47%)
  blocking collectives  24.2 us (22%)
  between operations  14.5 us (13%)
  other arithmetic  6.89 us (6%)
  matrix products  6.53 us (6%)
  local copies, waits for them, and re-layouts  5.81 us (5%)
    reduce_scatter x1, waiting for transfers between devices, per_device(): lax.psum_scatter(jnp.einsum('ijh,ikh->jkh', tri_rows, a_bf, preferred_ele...  31.1 us
    reduce_scatter x1, waiting for transfers between devices, per_device(): lax.psum_scatter(jnp.einsum('jkh,ikh->jih', b_every, a_bf, preferred_elem...  19.6 us
    all_gather x1, blocking collectives, per_device(): tri_rows = lax.all_gather(d_tri, 'col', axis=1, tiled=True)  13.4 us
    all_gather x1, blocking collectives, per_device(): b_every = lax.all_gather(b_bf, 'row', axis=0, tiled=True)  10.8 us
    all_gather x1, local copies, waits for them, and re-layouts, per_device(): b_every = lax.all_gather(b_bf, 'row', axis=0, tiled=True)  2.95 us
  transfers between devices with their start and end apart: 2, of which 2 were waited for; matrix products, arithmetic and copies ran while one was open for 1% of the time, Pallas kernels for 0%

commit v1 on v0

--- a/solution.py
+++ b/solution.py
@@ -69,7 +69,24 @@
     proj = jnp.dot(x_bf, w_proj, preferred_element_type=jnp.float32) + b_proj
     mask_f = pair_mask.astype(jnp.float32)[..., None]
     a_bf, b_bf = gate_pair(proj, mask_f)
-    b_every = lax.all_gather(b_bf, "row", axis=0, tiled=True)
+    peers, index, span = (lax.axis_size("row"), lax.axis_index("row"), b_bf.shape[0])
+    right = [(i, (i + 1) % peers) for i in range(peers)]
+    left = [(i, (i - 1) % peers) for i in range(peers)]
+    whole = jnp.zeros((*b_bf.shape[:0], peers * span, *b_bf.shape[0 + 1 :]), b_bf.dtype)
+    whole = lax.dynamic_update_slice_in_dim(whole, b_bf, index * span, axis=0)
+    from_left = from_right = b_bf
+    middle = peers // 2
+    for step in range(1, middle + 1):
+        from_left = lax.ppermute(from_left, "row", right)
+        whole = lax.dynamic_update_slice_in_dim(
+            whole, from_left, (index - step) % peers * span, axis=0
+        )
+        if step < peers - middle:
+            from_right = lax.ppermute(from_right, "row", left)
+            whole = lax.dynamic_update_slice_in_dim(
+                whole, from_right, (index + step) % peers * span, axis=0
+            )
+    b_every = whole
     owned = lax.psum_scatter(
         jnp.einsum("jkh,ikh->jih", b_every, a_bf, preferred_element_type=jnp.float32).astype(
             jnp.bfloat16

time: 109 us -> 268 us (2.46)
  local copies, waits for them, and re-layouts: 5.81 us -> 166 us
  blocking collectives: 24.2 us -> 13.4 us
  starting transfers between devices: 0.08 us -> 8.82 us
  waiting for transfers between devices: 50.7 us -> 58.1 us
  matrix products: 6.53 us -> 3.02 us
  other arithmetic: 6.89 us -> 3.99 us
    dynamic_update_slice x0 -> x8, local copies, waits for them, and re-layouts: none -> 157 us  [the longest x4 87.2 us: per_device(): lax.dynamic_update_slice_in_dim(whole, from_left, (index - step) % peers...]
    all_gather x1 -> x0, blocking collectives: 10.8 us -> none  [per_device(): b_every = lax.all_gather(b_bf, 'row', axis=0, tiled=True)]
    ppermute x0 -> x7, starting transfers between devices: none -> 8.74 us  [the longest x3 8.23 us: per_device(): from_right = lax.ppermute(from_right, 'row', left)]
    ppermute x0 -> x7, waiting for transfers between devices: none -> 4.73 us  [the longest x4 4.6 us: per_device(): from_left = lax.ppermute(from_left, 'row', right)]
    ppermute x0 -> x7, local copies, waits for them, and re-layouts: none -> 3.04 us  [the longest x4 1.74 us: per_device(): from_left = lax.ppermute(from_left, 'row', right)]
    all_gather x1 -> x0, local copies, waits for them, and re-layouts: 2.95 us -> none  [per_device(): b_every = lax.all_gather(b_bf, 'row', axis=0, tiled=True)]
  transfers between devices with their start and end apart: 2 -> 9, of which waited for: 2 -> 7; matrix products, arithmetic and copies ran while one was open for 1% -> 52% of each run, Pallas kernels for 0% -> 0%
where the time goes in v1:
time: 268 us
  local copies, waits for them, and re-layouts  166 us (62%)
  waiting for transfers between devices  58.1 us (22%)
  between operations  14.6 us (5%)
  blocking collectives  13.4 us (5%)
  starting transfers between devices  8.82 us (3%)
  other arithmetic  3.99 us (1%)
  matrix products  3.02 us (1%)
    dynamic_update_slice x4, local copies, waits for them, and re-layouts, per_device(): lax.dynamic_update_slice_in_dim(whole, from_left, (index - step) % peers...  87.2 us
    dynamic_update_slice x3, local copies, waits for them, and re-layouts, per_device(): lax.dynamic_update_slice_in_dim(whole, from_right, (index + step) % peers...  65.4 us
    reduce_scatter x1, waiting for transfers between devices, per_device(): lax.psum_scatter(jnp.einsum('ijh,ikh->jkh', tri_rows, a_bf, preferred_ele...  31.5 us
    reduce_scatter x1, waiting for transfers between devices, per_device(): lax.psum_scatter(jnp.einsum('jkh,ikh->jih', b_every, a_bf, preferred_elem...  21.8 us
    all_gather x1, blocking collectives, per_device(): tri_rows = lax.all_gather(d_tri, 'col', axis=1, tiled=True)  13.4 us
    ppermute x3, starting transfers between devices, per_device(): from_right = lax.ppermute(from_right, 'row', left)  8.23 us
  transfers between devices with their start and end apart: 9, of which 7 were waited for; matrix products, arithmetic and copies ran while one was open for 52% of the time, Pallas kernels for 0%

profile of v1, /device:TPU:0, one launch (start us, length us, event | category | flops | bytes accessed | tf_op | source)
XLA Modules:
  0.0 268.0 jit_solution(12103794651261011457)
XLA Ops:
  7.2 0.9 convert_reduce_fusion
  10.5 2.9 %collective-permute-start.1 = (bf16[8,16,128]{2,1,0:T(8,128)(2,1)S(1)}, bf16[8,16,128]{2,1,0:T(8,128)(2,1)S(1)}, u32[]{:S(2)}, u32[]{:S(2)}) collective-permute-start(bf16[8,16,128]{2,1,0:T(8,128)(2,1)S(1)} %get-tuple-element.12), channel_id=1, source_target_pairs={{0,28},{4,0},{8,4},{12,8},{16,12},{20,16},{24,20},{28,24},{1,29},{... | collective-permute-start | bytes 98312 | tf_op jit(solution)/shard_map/ppermute | solution.py:85
  13.5 1.5 collective-permute-done
  15.1 2.6 collective-permute-start.3
  17.7 1.5 collective-permute-done.2
  19.3 2.6 collective-permute-start.5
  21.9 1.5 collective-permute-done.4
  24.3 4.6 %dynamic_update_slice.24 = bf16[64,16,128]{0,1,2:T(8,128)(2,1)S(1)} dynamic-update-slice(bf16[64,16,128]{0,1,2:T(8,128)(2,1)S(1)} %broadcast_in_dim.2, bf16[8,16,128]{0,1,2:T(8,128)(2,1)S(1)} %copy.29, s32[]{:T(128)S(6)} %select_n.55, s32[]{:T(128)} %constant.69.clone.1, s32[]{:T(128)} %constant.69.clone.1) | dynamic-update-slice | bytes 65540 | tf_op jit(solution)/shard_map/dynamic_update_slice | solution.py:76
  29.4 21.8 %dynamic_update_slice.25 = bf16[64,16,128]{0,1,2:T(8,128)(2,1)S(1)} dynamic-update-slice(bf16[64,16,128]{0,1,2:T(8,128)(2,1)S(1)} %dynamic_update_slice.24, bf16[8,16,128]{0,1,2:T(8,128)(2,1)S(1)} %copy.30, s32[]{:T(128)S(6)} %select_n.57, s32[]{:T(128)} %constant.69.clone.1, s32[]{:T(128)} %constant.69.clone.1) | dynamic-update-slice | bytes 65540 | tf_op jit(solution)/shard_map/dynamic_update_slice | solution.py:81
  51.7 21.8 %dynamic_update_slice.26 = bf16[64,16,128]{0,1,2:T(8,128)(2,1)S(1)} dynamic-update-slice(bf16[64,16,128]{0,1,2:T(8,128)(2,1)S(1)} %dynamic_update_slice.25, bf16[8,16,128]{0,1,2:T(8,128)(2,1)S(1)} %copy.31, s32[]{:T(128)S(6)} %select_n.59, s32[]{:T(128)} %constant.69.clone.1, s32[]{:T(128)} %constant.69.clone.1) | dynamic-update-slice | bytes 65540 | tf_op jit(solution)/shard_map/dynamic_update_slice | solution.py:86
  73.9 21.8 %dynamic_update_slice.27 = bf16[64,16,128]{0,1,2:T(8,128)(2,1)S(1)} dynamic-update-slice(bf16[64,16,128]{0,1,2:T(8,128)(2,1)S(1)} %dynamic_update_slice.26, bf16[8,16,128]{0,1,2:T(8,128)(2,1)S(1)} %copy.32, s32[]{:T(128)S(6)} %select_n.61, s32[]{:T(128)} %constant.69.clone.1, s32[]{:T(128)} %constant.69.clone.1) | dynamic-update-slice | bytes 65540 | tf_op jit(solution)/shard_map/dynamic_update_slice | solution.py:81
  96.2 21.8 %dynamic_update_slice.28 = bf16[64,16,128]{0,1,2:T(8,128)(2,1)S(1)} dynamic-update-slice(bf16[64,16,128]{0,1,2:T(8,128)(2,1)S(1)} %dynamic_update_slice.27, bf16[8,16,128]{0,1,2:T(8,128)(2,1)S(1)} %copy.33, s32[]{:T(128)S(6)} %select_n.63, s32[]{:T(128)} %constant.69.clone.1, s32[]{:T(128)} %constant.69.clone.1) | dynamic-update-slice | bytes 65540 | tf_op jit(solution)/shard_map/dynamic_update_slice | solution.py:86
  118.4 21.8 %dynamic_update_slice.29 = bf16[64,16,128]{0,1,2:T(8,128)(2,1)S(1)} dynamic-update-slice(bf16[64,16,128]{0,1,2:T(8,128)(2,1)S(1)} %dynamic_update_slice.28, bf16[8,16,128]{0,1,2:T(8,128)(2,1)S(1)} %copy.34, s32[]{:T(128)S(6)} %select_n.65, s32[]{:T(128)} %constant.69.clone.1, s32[]{:T(128)} %constant.69.clone.1) | dynamic-update-slice | bytes 65540 | tf_op jit(solution)/shard_map/dynamic_update_slice | solution.py:81
  140.7 21.8 %dynamic_update_slice.30 = bf16[64,16,128]{0,1,2:T(8,128)(2,1)S(1)} dynamic-update-slice(bf16[64,16,128]{0,1,2:T(8,128)(2,1)S(1)} %dynamic_update_slice.29, bf16[8,16,128]{0,1,2:T(8,128)(2,1)S(1)} %copy.35, s32[]{:T(128)S(6)} %select_n.67, s32[]{:T(128)} %constant.69.clone.1, s32[]{:T(128)} %constant.69.clone.1) | dynamic-update-slice | bytes 65540 | tf_op jit(solution)/shard_map/dynamic_update_slice | solution.py:86
  163.0 21.8 %dynamic_update_slice.31 = bf16[64,16,128]{0,1,2:T(8,128)(2,1)S(1)} dynamic-update-slice(bf16[64,16,128]{0,1,2:T(8,128)(2,1)S(1)} %dynamic_update_slice.30, bf16[8,16,128]{0,1,2:T(8,128)(2,1)S(1)} %copy.36, s32[]{:T(128)S(6)} %select_n.69, s32[]{:T(128)} %constant.69.clone.1, s32[]{:T(128)} %constant.69.clone.1) | dynamic-update-slice | bytes 65540 | tf_op jit(solution)/shard_map/dynamic_update_slice | solution.py:81
  185.1 0.9 copy.38
  186.0 21.8 %reduce-scatter.3.cloned.1.call-done = bf16[16,8,128]{2,1,0:T(8,128)(2,1)} async-done(((bf16[64,8,128]{2,1,0:T(8,128)(2,1)}), bf16[16,8,128]{2,1,0:T(8,128)(2,1)}) %reduce-scatter.3.cloned.1.call-update) | async-done | bytes 32784 | tf_op jit(solution)/shard_map/reduce_scatter | solution.py:90
  207.9 0.9 bitcast_reduce_fusion
  210.4 0.9 multiply_convert_fusion.4
  211.7 13.4 %all_gather.3 = bf16[8,64,128]{2,0,1:T(8,128)(2,1)S(1)} all-gather(bf16[8,16,128]{2,0,1:T(8,128)(2,1)S(1)} %copy.40), channel_id=1, replica_groups=mesh['row'=8,'col'=4] {'col'}, dimensions={1}, use_global_device_ids=true | all-gather | bytes 163840 | tf_op jit(solution)/shard_map/all_gather | solution.py:109
  225.7 1.3 copy.45
  227.6 31.5 %reduce-scatter.5.cloned.1.call-done = bf16[8,16,128]{2,1,0:T(8,128)(2,1)} async-done(((bf16[64,16,128]{2,1,0:T(8,128)(2,1)}), bf16[8,16,128]{2,1,0:T(8,128)(2,1)}) %reduce-scatter.5.cloned.1.call-update) | async-done | bytes 32784 | tf_op jit(solution)/shard_map/reduce_scatter | solution.py:111
  259.0 0.9 multiply_convert_fusion.3
  260.4 0.8 fusion.25
  (73 shorter events, 10.2 us)
Async XLA Ops:
  7.2 1.8 copy-start
  7.2 0.9 copy-start.1
  7.2 200.7 %reduce-scatter.3.cloned.1.call-start = ((), (), s32[]{:S(2)}) async-start(), calls=%async_computation.2 | async-start | bytes 163840 | tf_op jit(solution)/shard_map/reduce_scatter | solution.py:90
  8.3 0.7 copy-start.6
  9.0 0.7 copy-start.7
  9.0 0.7 copy-start.8
  9.0 0.7 copy-start.9
  10.0 5.0 %collective-permute-start = (bf16[8,16,128]{2,1,0:T(8,128)(2,1)S(1)}, bf16[8,16,128]{2,1,0:T(8,128)(2,1)S(1)}, u32[]{:S(2)}, u32[]{:S(2)}) collective-permute-start(bf16[8,16,128]{2,1,0:T(8,128)(2,1)S(1)} %get-tuple-element.12), channel_id=1, source_target_pairs={{0,4},{4,8},{8,12},{12,16},{16,20},{20,24},{24,28},{28,0},{1,5},{5... | collective-permute-start | bytes 98312 | tf_op jit(solution)/shard_map/ppermute | solution.py:80
  10.5 4.5 %collective-permute-start.1 = (bf16[8,16,128]{2,1,0:T(8,128)(2,1)S(1)}, bf16[8,16,128]{2,1,0:T(8,128)(2,1)S(1)}, u32[]{:S(2)}, u32[]{:S(2)}) collective-permute-start(bf16[8,16,128]{2,1,0:T(8,128)(2,1)S(1)} %get-tuple-element.12), channel_id=1, source_target_pairs={{0,28},{4,0},{8,4},{12,8},{16,12},{20,16},{24,20},{28,24},{1,29},{... | collective-permute-start | bytes 98312 | tf_op jit(solution)/shard_map/ppermute | solution.py:85
  15.0 4.2 %collective-permute-start.2 = (bf16[8,16,128]{2,1,0:T(8,128)(2,1)S(1)}, bf16[8,16,128]{2,1,0:T(8,128)(2,1)S(1)}, u32[]{:S(2)}, u32[]{:S(2)}) collective-permute-start(bf16[8,16,128]{2,1,0:T(8,128)(2,1)S(1)} %collective-permute-done), channel_id=1, source_target_pairs={{0,4},{4,8},{8,12},{12,16},{16,20},{20,24},{24,28},{28,0},{1,5},{5... | collective-permute-start | bytes 98312 | tf_op jit(solution)/shard_map/ppermute | solution.py:80
  15.1 4.2 %collective-permute-start.3 = (bf16[8,16,128]{2,1,0:T(8,128)(2,1)S(1)}, bf16[8,16,128]{2,1,0:T(8,128)(2,1)S(1)}, u32[]{:S(2)}, u32[]{:S(2)}) collective-permute-start(bf16[8,16,128]{2,1,0:T(8,128)(2,1)S(1)} %collective-permute-done.1), channel_id=1, source_target_pairs={{0,28},{4,0},{8,4},{12,8},{16,12},{20,16},{24,20},{28,24},{1,29},{... | collective-permute-start | bytes 98312 | tf_op jit(solution)/shard_map/ppermute | solution.py:85
  19.2 4.2 %collective-permute-start.4 = (bf16[8,16,128]{2,1,0:T(8,128)(2,1)S(1)}, bf16[8,16,128]{2,1,0:T(8,128)(2,1)S(1)}, u32[]{:S(2)}, u32[]{:S(2)}) collective-permute-start(bf16[8,16,128]{2,1,0:T(8,128)(2,1)S(1)} %collective-permute-done.2), channel_id=1, source_target_pairs={{0,4},{4,8},{8,12},{12,16},{16,20},{20,24},{24,28},{28,0},{1,5},{5... | collective-permute-start | bytes 98312 | tf_op jit(solution)/shard_map/ppermute | solution.py:80
  19.3 121.0 %collective-permute-start.5 = (bf16[8,16,128]{2,1,0:T(8,128)(2,1)S(1)}, bf16[8,16,128]{2,1,0:T(8,128)(2,1)S(1)}, u32[]{:S(2)}, u32[]{:S(2)}) collective-permute-start(bf16[8,16,128]{2,1,0:T(8,128)(2,1)S(1)} %collective-permute-done.3), channel_id=1, source_target_pairs={{0,28},{4,0},{8,4},{12,8},{16,12},{20,16},{24,20},{28,24},{1,29},{... | collective-permute-start | bytes 98312 | tf_op jit(solution)/shard_map/ppermute | solution.py:85
  23.5 139.1 %collective-permute-start.6 = (bf16[8,16,128]{2,1,0:T(8,128)(2,1)S(1)}, bf16[8,16,128]{2,1,0:T(8,128)(2,1)S(1)}, u32[]{:S(2)}, u32[]{:S(2)}) collective-permute-start(bf16[8,16,128]{2,1,0:T(8,128)(2,1)S(1)} %collective-permute-done.4), channel_id=1, source_target_pairs={{0,4},{4,8},{8,12},{12,16},{16,20},{20,24},{24,28},{28,0},{1,5},{5... | collective-permute-start | bytes 98312 | tf_op jit(solution)/shard_map/ppermute | solution.py:80
  186.0 73.1 %reduce-scatter.5.cloned.1.call-start = ((), (), s32[]{:S(2)}) async-start(), calls=%async_computation.3 | async-start | bytes 294912 | tf_op jit(solution)/shard_map/reduce_scatter | solution.py:111
  207.9 0.9 copy-start.2
  208.8 0.8 copy-start.4
  209.0 0.7 copy-start.10
  209.0 0.7 copy-start.11
  209.0 0.7 copy-start.12
  209.7 0.8 copy-start.5
  209.7 0.8 copy-start.13
  210.4 0.9 copy-start.3
Sparse Core Ops, SparseCore 0:
  186.1 21.7 reduce-scatter.2
  227.1 31.8 reduce-scatter.4
